TPU v7x, 128 devices: a whole 4x4x4 slice. The times are simulated.
128 devices in a mesh: queue: 32 (over y, x, z_lo), head: 4 (over z_hi, core).
Axes of the slice: x: 4, y: 4, z: 4 (z_hi: 2, z_lo: 2; z = z_hi * 2 + z_lo), core: 2. Of those that a mesh axis runs over, the one named last changes fastest.
Arguments:
- latents: bfloat16 [64, 384, 5120], P('queue'), may hold values from -6 to 6
- control: bfloat16 [64, 384, 5120], P('queue'), may hold values from -3 to 3
- levels: int32 [64], P('queue'), may hold values from 0 to 63
- window_mask: int32 [64, 2], P('queue'), may hold values 0 or 1
- modulation: float32 [64, 3, 5120], replicated, may hold values from -3 to 3
- w_query: bfloat16 [5120, 2560], P('queue', 'head'), may hold values from -1 to 1
- w_key: bfloat16 [5120, 2560], P('queue', 'head'), may hold values from -1 to 1
- w_value: bfloat16 [5120, 2560], P('queue', 'head'), may hold values from -0.078125 to 0.078125
- w_out: bfloat16 [2560, 5120], P('head', 'queue'), may hold values from -0.125 to 0.125
- q_gain: float32 [2560], P('head'), may hold values from 0.6 to 8
- k_gain: float32 [2560], P('head'), may hold values from 0.6 to 8
Outputs:
- next_queue: float32 [64, 384, 5120], P('queue', None, 'head')
All inputs are finite; a program needn't handle non-finite values. No bound on the sum of `window_mask` on one device may be relied on, other than what follows from the above.
Results may differ from a plain program's by a relative error of at most 0.019.
The roundings to bfloat16 on the way count: a program that leaves them out, or rounds other values in their place, can miss the bound.
Values may be sent and summed in bfloat16 or wider, within the bound.
A program may use at most 192 MiB of HBM per device.

v0:
```python
import jax
import jax.numpy as jnp
from jax import lax
from jax.sharding import PartitionSpec as P

HD = 128


def from_behind(value, axis, by):
    peers = lax.axis_size(axis)
    pairs = [(i, i + by) for i in range(peers) if 0 <= i + by < peers]
    return lax.ppermute(value, axis, pairs)


def shifted(value, axis, steps):
    count = lax.axis_size(axis)
    pairs = [(source, (source + steps) % count) for source in range(count)]
    return lax.ppermute(value, axis, pairs)


def layer_norm(hidden):
    center = hidden - jnp.mean(hidden, axis=-1, keepdims=True)
    variance = jnp.mean(center * center, axis=-1, keepdims=True)
    return center * lax.rsqrt(variance + 1e-06)


def apply_gain(values, square_sum, total_width, gain):
    floats = values.astype(jnp.float32)
    return (floats * lax.rsqrt(square_sum[:, None] / total_width + 1e-06) * gain).astype(
        jnp.bfloat16
    )


def row_squares(values):
    floats = values.astype(jnp.float32)
    return jnp.sum(floats * floats, axis=-1)


def shards(
    latents,
    control,
    levels,
    window_mask,
    modulation,
    w_query,
    w_key,
    w_value,
    w_out,
    q_gain,
    k_gain,
):
    nchunk, row_count, model_width = latents.shape
    level_count = modulation.shape[0]
    local_cols = w_query.shape[1]
    heads_local = local_cols // HD
    head_count = lax.axis_size("head")
    total_width = local_cols * head_count
    owner_index = lax.axis_index("queue")
    head_index = lax.axis_index("head")
    first_span = owner_index * nchunk
    hidden = latents.astype(jnp.float32) + control.astype(jnp.float32)
    onehot = (levels[:, None] == jnp.arange(level_count, dtype=jnp.int32)[None, :]).astype(
        jnp.float32
    )
    level_mods = jnp.dot(
        onehot, modulation.reshape(level_count, 3 * model_width), precision=lax.Precision.HIGHEST
    ).reshape(nchunk, 3, model_width)
    normed = (
        layer_norm(hidden) * (1.0 + level_mods[:, 1][:, None, :]) + level_mods[:, 0][:, None, :]
    ).astype(jnp.bfloat16)
    flat_rows = normed.reshape(nchunk * row_count, model_width)
    row_total = nchunk * row_count
    pieces = (
        lax.all_gather(w_query, "queue", axis=0, tiled=True),
        lax.all_gather(w_key, "queue", axis=0, tiled=True),
        lax.all_gather(w_value, "queue", axis=0, tiled=True),
    )
    query, keyproj, valueproj = tuple(
        (
            jnp.dot(flat_rows, piece_rows, preferred_element_type=jnp.float32)
            for piece_rows in pieces
        )
    )
    query = query.astype(jnp.bfloat16)
    keyproj = keyproj.astype(jnp.bfloat16)
    valueproj = valueproj.astype(jnp.bfloat16)
    query_sq, key_sq = lax.psum((row_squares(query), row_squares(keyproj)), "head")
    qhat = apply_gain(query, query_sq, total_width, q_gain)
    own_keys = apply_gain(keyproj, key_sq, total_width, k_gain)
    prior_keys, prior_values = from_behind((own_keys, valueproj), "queue", 1)
    key_stack = jnp.concatenate([prior_keys, own_keys], axis=0).reshape(
        2 * nchunk, row_count, heads_local, HD
    )
    value_stack = jnp.concatenate([prior_values, valueproj], axis=0).reshape(
        2 * nchunk, row_count, heads_local, HD
    )
    key_windows = jnp.stack(
        [
            key_stack[nchunk + index_span - 2 : nchunk + index_span + 1]
            for index_span in range(nchunk)
        ]
    ).reshape(nchunk, 3 * row_count, heads_local, HD)
    value_windows = jnp.stack(
        [
            value_stack[nchunk + index_span - 2 : nchunk + index_span + 1]
            for index_span in range(nchunk)
        ]
    ).reshape(nchunk, 3 * row_count, heads_local, HD)
    span_ids = first_span + jnp.arange(nchunk, dtype=jnp.int32)
    seen_far = (window_mask[:, 0] == 1) & (span_ids >= 2)
    seen_near = (window_mask[:, 1] == 1) & (span_ids >= 1)
    seen = jnp.stack([seen_far, seen_near, jnp.ones((nchunk,), dtype=bool)], axis=1)
    key_seen = jnp.repeat(seen, row_count, axis=1)
    query_spans = qhat.reshape(nchunk, row_count, heads_local, HD)
    scores = jnp.einsum(
        "cqhd,ckhd->chqk", query_spans, key_windows, preferred_element_type=jnp.float32
    ) * HD ** (-0.5)
    scores = jnp.where(key_seen[:, None, None, :], scores, -1e30)
    top = jnp.max(scores, axis=-1, keepdims=True)
    expo = jnp.exp(scores - top)
    prob_bf = (expo / jnp.sum(expo, axis=-1, keepdims=True)).astype(jnp.bfloat16)
    attended = jnp.einsum(
        "chqk,ckhd->cqhd", prob_bf, value_windows, preferred_element_type=jnp.float32
    )
    attended = attended.astype(jnp.bfloat16).reshape(row_total, local_cols)
    partial_out = jnp.dot(
        attended,
        lax.all_gather(w_out, "queue", axis=1, tiled=True),
        preferred_element_type=jnp.float32,
    )
    col_width = model_width // head_count
    hidden_cols = lax.dynamic_slice_in_dim(hidden, head_index * col_width, col_width, 2)
    gate_cols = lax.dynamic_slice_in_dim(level_mods[:, 2], head_index * col_width, col_width, 1)
    branch = (
        lax.psum_scatter(partial_out.astype(jnp.bfloat16), "head", scatter_dimension=1, tiled=True)
        .astype(jnp.float32)
        .reshape(nchunk, row_count, col_width)
    )
    updated = hidden_cols + gate_cols[:, None, :] * branch
    arrived = shifted(updated[nchunk - 1].astype(jnp.bfloat16), "queue", 1).astype(jnp.float32)
    return jnp.concatenate([arrived[None], updated[: nchunk - 1]], axis=0)


def solution(mesh):
    placed = (
        P("queue", None, None),
        P("queue", None, None),
        P("queue"),
        P("queue", None),
        P(),
        P("queue", "head"),
        P("queue", "head"),
        P("queue", "head"),
        P("head", "queue"),
        P("head"),
        P("head"),
    )
    return jax.shard_map(
        shards, mesh=mesh, in_specs=placed, out_specs=P("queue", None, "head"), check_vma=False
    )
```

profile of v0, /device:TPU:0, one launch (start us, length us, event | category | flops | bytes accessed | tf_op | source)
XLA Modules:
  0.0 834.2 jit_solution(3768649909468280332)
XLA Ops:
  6.5 0.7 all-gather.7.cloned.1.call-update
  7.3 0.7 all-gather.9.cloned.1.call-update
  8.1 0.7 all-gather.5.cloned.1.call-update
  8.8 0.5 all-gather.11.cloned.1.call-update
  9.3 0.0 reduce-scatter.2.cloned.1.call-start
  9.4 13.7 %convert_add_fusion = (f32[2,384,5120]{2,1,0:T(8,128)}, f32[2,384]{1,0:T(2,128)S(1)}) fusion(bf16[2,384,5120]{2,1,0:T(8,128)(2,1)} %param.12, bf16[2,384,5120]{2,1,0:T(8,128)(2,1)} %param.11), kind=kLoop, calls=%fused_computation.6 | loop fusion | flops 15727872 | bytes 31460352 | tf_op jit(solution)/shard_map/add | solution.py:61
  23.1 6.4 multiply_reduce_fusion
  29.5 0.1 compare_and_fusion.1
  29.6 0.1 pad.8.clone
  29.7 0.1 add_add_fusion
  29.8 3.5 fusion.6
  33.3 10.8 %add_convert_fusion = bf16[2,384,5120]{2,1,0:T(8,128)(2,1)} fusion(f32[2,5120]{1,0:T(2,128)S(1)} %get-tuple-element.14, f32[2,5120]{1,0:T(2,128)S(1)} %get-tuple-element.15, f32[2,384]{1,0:T(2,128)S(1)} %add_rsqrt_fusion.2, f32[2,384]{1,0:T(2,128)S(1)} %broadcast_multiply_fusion, bf16[2,384,5120]{2,1,0:T(8,128)(2,1)} %param.12, bf16[2,384,5120]{2,1,0:T(8,128)(2,1)} %param.11), kind=kLoop, calls=%fused_computation.4 | loop fusion | flops 31457280 | bytes 23681024 | tf_op jit(solution)/shard_map/convert_element_type | solution.py:70
  44.1 132.3 %all-gather.7.cloned.1.call-done = bf16[5120,640]{1,0:T(8,128)(2,1)} async-done(((bf16[160,640]{1,0:T(8,128)(2,1)}), bf16[5120,640]{1,0:T(8,128)(2,1)}) %all-gather.7.cloned.1.call-update) | async-done | bytes 6553616 | tf_op jit(solution)/shard_map/all_gather | solution.py:74
  176.4 10.4 %fusion.17 = (f32[768]{0:T(1024)S(1)}, bf16[768,640]{0,1:T(8,128)(2,1)S(1)}) fusion(bf16[768,5120]{1,0:T(8,128)(2,1)} %bitcast.59, bf16[5120,640]{1,0:T(8,128)(2,1)} %all-gather.7.cloned.1.call-done), kind=kOutput, calls=%fused_computation.30 | convolution fusion | flops 5035129856 | bytes 15404032 | tf_op jit(solution)/shard_map/dot_general | solution.py:80
  186.8 153.5 %all-gather.9.cloned.1.call-done = bf16[5120,640]{1,0:T(8,128)(2,1)} async-done(((bf16[160,640]{1,0:T(8,128)(2,1)}), bf16[5120,640]{1,0:T(8,128)(2,1)}) %all-gather.9.cloned.1.call-update) | async-done | bytes 6553616 | tf_op jit(solution)/shard_map/all_gather | solution.py:75
  340.4 10.6 %fusion.20 = (f32[768]{0:T(1024)S(1)}, bf16[768,640]{1,0:T(8,128)(2,1)S(1)}) fusion(bf16[768,5120]{1,0:T(8,128)(2,1)} %bitcast.60, bf16[5120,640]{1,0:T(8,128)(2,1)} %all-gather.9.cloned.1.call-done), kind=kOutput, calls=%fused_computation.33 | convolution fusion | flops 5035129856 | bytes 15404032 | tf_op jit(solution)/shard_map/dot_general | solution.py:80
  351.0 7.7 all-reduce
  358.7 0.3 fusion.22
  359.1 2.4 collective-permute-start.1
  361.4 163.7 %all-gather.5.cloned.1.call-done = bf16[5120,640]{1,0:T(8,128)(2,1)} async-done(((bf16[160,640]{1,0:T(8,128)(2,1)}), bf16[5120,640]{1,0:T(8,128)(2,1)}) %all-gather.5.cloned.1.call-update) | async-done | bytes 6553616 | tf_op jit(solution)/shard_map/all_gather | solution.py:76
  525.1 11.3 %convolution_convert_fusion.3 = bf16[768,640]{1,0:T(8,128)(2,1)} fusion(bf16[768,5120]{1,0:T(8,128)(2,1)} %bitcast.61, bf16[5120,640]{1,0:T(8,128)(2,1)} %all-gather.5.cloned.1.call-done), kind=kOutput, calls=%fused_computation.48 | convolution fusion | flops 5033656320 | bytes 15400960 | tf_op jit(solution)/shard_map/dot_general | solution.py:80
  536.4 2.5 collective-permute-start
  538.9 0.1 broadcast_bitcast_fusion
  539.0 0.3 fusion.19
  539.3 1.2 reshape.85
  540.5 2.0 fusion.27
  542.5 2.1 copy.21
  544.6 3.6 copy.23
  548.2 0.9 copy.22
  549.1 2.1 copy.24
  551.2 12.5 %collective-permute-done = bf16[768,640]{1,0:T(8,128)(2,1)} collective-permute-done((bf16[768,640]{1,0:T(8,128)(2,1)}, bf16[768,640]{1,0:T(8,128)(2,1)}, u32[]{:S(2)}, u32[]{:S(2)}) %collective-permute-start) | collective-permute-done | bytes 983072 | tf_op jit(solution)/shard_map/ppermute | solution.py:12
  563.8 2.0 fusion.28
  565.8 2.2 copy.19
  568.0 0.9 copy.20
  569.0 14.5 %fusion.56 = (f32[2,5,384]{2,1,0:T(8,128)S(1)}, f32[2,5,384,1152]{3,2,1,0:T(8,128)}) fusion(pred[2,1152]{1,0:T(4,128)(4,1)S(1)} %bitcast.69, bf16[1,1152,5,128]{3,1,2,0:T(8,128)(2,1)} %copy.24, bf16[1,1152,5,128]{3,1,2,0:T(8,128)(2,1)} %copy.23, bf16[2,384,5,128]{1,0,3,2:T(2,128)(2,1)} %reshape.85), kind=kOutput, calls=%fused_computation.78 | convolution fusion | flops 1151632512 | bytes 21644544 | tf_op jit(solution)/shard_map/sub | solution.py:120
  583.5 7.8 fusion.32
  591.3 1.0 copy.26
  592.3 0.2 copy.30
  592.5 114.0 %all-gather.11.cloned.1.call-done = bf16[640,5120]{0,1:T(8,128)(2,1)} async-done(((bf16[640,160]{0,1:T(8,128)(2,1)}), bf16[640,5120]{0,1:T(8,128)(2,1)}) %all-gather.11.cloned.1.call-update) | async-done | bytes 6553616 | tf_op jit(solution)/shard_map/all_gather | solution.py:128
  706.4 11.4 %convolution_convert_fusion = bf16[768,5120]{1,0:T(8,128)(2,1)} fusion(bf16[768,640]{0,1:T(8,128)(2,1)S(1)} %bitcast.68, bf16[640,5120]{0,1:T(8,128)(2,1)} %all-gather.11.cloned.1.call-done), kind=kOutput, calls=%fused_computation.12 | convolution fusion | flops 5037096960 | bytes 15400960 | tf_op jit(solution)/shard_map/dot_general | solution.py:126
  717.9 76.6 %reduce-scatter.2.cloned.1.call-done = bf16[768,1280]{1,0:T(8,128)(2,1)} async-done(((bf16[768,5120]{1,0:T(8,128)(2,1)}), bf16[768,1280]{1,0:T(8,128)(2,1)}) %reduce-scatter.2.cloned.1.call-update) | async-done | bytes 1966096 | tf_op jit(solution)/shard_map/reduce_scatter | solution.py:135
  794.6 3.1 fusion.9
  797.7 0.1 fusion.35
  797.8 0.7 collective-permute-start.2
  798.5 0.1 slice.57
  798.6 26.8 %collective-permute-done.2 = bf16[384,1280]{1,0:T(8,128)(2,1)S(1)} collective-permute-done((bf16[384,1280]{1,0:T(8,128)(2,1)S(1)}, bf16[384,1280]{1,0:T(8,128)(2,1)S(1)}, u32[]{:S(2)}, u32[]{:S(2)}) %collective-permute-start.2) | collective-permute-done | bytes 983072 | tf_op jit(solution)/shard_map/ppermute | solution.py:18
  825.4 0.1 bitcast_convert_fusion
  825.5 2.2 pad_maximum_fusion
  (30 shorter events, 0.3 us)
Async XLA Ops:
  6.5 169.8 %all-gather.7.cloned.1.call-start = ((), (), s32[]{:S(2)}) async-start(), calls=%async_computation.2 | async-start | bytes 6758400 | tf_op jit(solution)/shard_map/all_gather | solution.py:74
  7.3 333.1 %all-gather.9.cloned.1.call-start = ((), (), s32[]{:S(2)}) async-start(), calls=%async_computation.3 | async-start | bytes 6758400 | tf_op jit(solution)/shard_map/all_gather | solution.py:75
  8.0 517.1 %all-gather.5.cloned.1.call-start = ((), (), s32[]{:S(2)}) async-start(), calls=%async_computation.1 | async-start | bytes 6758400 | tf_op jit(solution)/shard_map/all_gather | solution.py:76
  8.7 697.7 %all-gather.11.cloned.1.call-start = ((), (), s32[]{:S(2)}) async-start(), calls=%async_computation.4 | async-start | bytes 6758400 | tf_op jit(solution)/shard_map/all_gather | solution.py:128
  9.3 785.2 %reduce-scatter.2.cloned.1.call-start = ((), (), s32[]{:S(2)}) async-start(), calls=%async_computation.5 | async-start | bytes 9830400 | tf_op jit(solution)/shard_map/reduce_scatter | solution.py:135
  9.4 13.7 %slice-start = ((s8[7864320]{0:T(1024)(128)(4,1)}), s8[4194304]{0:T(1024)(128)(4,1)S(1)}, s32[]{:S(2)}) async-start(s8[7864320]{0:T(1024)(128)(4,1)} %bitcast.57), calls=%async_computation.6 | async-start | bytes 8388608
  9.4 13.7 %slice-start.1 = ((s8[7864320]{0:T(1024)(128)(4,1)}), s8[3670016]{0:T(1024)(128)(4,1)S(1)}, s32[]{:S(2)}) async-start(s8[7864320]{0:T(1024)(128)(4,1)} %bitcast.57), calls=%async_computation.7 | async-start | bytes 7340032
  23.1 6.4 copy-start.4
  23.1 6.7 copy-start.5
  186.8 171.9 %copy-start.2 = (f32[640]{0:T(1024)S(1)}, f32[640]{0:T(1024)}, u32[]{:S(2)}) copy-start(f32[640]{0:T(1024)} %param.21) | copy-start | bytes 7684
  359.0 177.3 %copy-start = (bf16[768,640]{1,0:T(8,128)(2,1)}, bf16[768,640]{1,0:T(8,128)(2,1)S(1)}, u32[]{:S(2)}) copy-start(bf16[768,640]{1,0:T(8,128)(2,1)S(1)} %fusion.22) | copy-start | bytes 2949124
  359.0 179.9 %copy-start.3 = (f32[640]{0:T(1024)S(1)}, f32[640]{0:T(1024)}, u32[]{:S(2)}) copy-start(f32[640]{0:T(1024)} %param.20) | copy-start | bytes 7684
  359.1 181.4 %collective-permute-start.1 = (bf16[768,640]{1,0:T(8,128)(2,1)S(1)}, bf16[768,640]{1,0:T(8,128)(2,1)}, u32[]{:S(2)}, u32[]{:S(2)}) collective-permute-start(bf16[768,640]{1,0:T(8,128)(2,1)S(1)} %fusion.22), channel_id=1, source_target_pairs={{0,4},{4,8},{8,12},{12,16},{16,20},{20,24},{24,28},{28,32},{32,36}... | collective-permute-start | bytes 2949128 | tf_op jit(solution)/shard_map/ppermute | solution.py:12
  536.4 27.4 %collective-permute-start = (bf16[768,640]{1,0:T(8,128)(2,1)}, bf16[768,640]{1,0:T(8,128)(2,1)}, u32[]{:S(2)}, u32[]{:S(2)}) collective-permute-start(bf16[768,640]{1,0:T(8,128)(2,1)} %convolution_convert_fusion.3), channel_id=1, source_target_pairs={{0,4},{4,8},{8,12},{12,16},{16,20},{20,24},{24,28},{28,32},{32,36}... | collective-permute-start | bytes 2949128 | tf_op jit(solution)/shard_map/ppermute | solution.py:12
  569.0 14.5 %copy-start.1 = (bf16[1152,640]{0,1:T(8,128)(2,1)S(1)}, bf16[1152,640]{0,1:T(8,128)(2,1)}, u32[]{:S(2)}) copy-start(bf16[1152,640]{0,1:T(8,128)(2,1)} %copy.19) | copy-start | bytes 4423684
  797.8 27.6 %collective-permute-start.2 = (bf16[384,1280]{1,0:T(8,128)(2,1)S(1)}, bf16[384,1280]{1,0:T(8,128)(2,1)S(1)}, u32[]{:S(2)}, u32[]{:S(2)}) collective-permute-start(bf16[384,1280]{1,0:T(8,128)(2,1)S(1)} %fusion.35), channel_id=1, source_target_pairs={{0,4},{4,8},{8,12},{12,16},{16,20},{20,24},{24,28},{28,32},{32,36}... | collective-permute-start | bytes 2949128 | tf_op jit(solution)/shard_map/ppermute | solution.py:18
Sparse Core Ops, SparseCore 0:
  9.0 167.3 all-gather.6
  178.0 162.3 all-gather.8
  342.0 183.0 all-gather.4
  526.6 179.8 all-gather.10
  718.0 76.5 reduce-scatter.1
where the time goes:
time: 835 us; the launch traced here: 834 us
  waiting for transfers between devices  682 us (82%)
  matrix products  69.5 us (8%)
  other arithmetic  41.2 us (5%)
  local copies, waits for them, and re-layouts  14.7 us (2%)
  between operations  13.4 us (2%)
    all_gather x1, waiting for transfers between devices, shards(): lax.all_gather(w_value, 'queue', axis=0, tiled=True)  164 us
    all_gather x1, waiting for transfers between devices, shards(): lax.all_gather(w_key, 'queue', axis=0, tiled=True)  154 us
    all_gather x1, waiting for transfers between devices, shards(): lax.all_gather(w_query, 'queue', axis=0, tiled=True)  132 us
    all_gather x1, waiting for transfers between devices, shards(): lax.all_gather(w_out, 'queue', axis=1, tiled=True)  114 us
    reduce_scatter x1, waiting for transfers between devices, shards(): lax.psum_scatter(partial_out.astype(jnp.bfloat16), 'head', scatter_dimens...  76.6 us
    dot_general x3, matrix products, shards(): jnp.dot(flat_rows, piece_rows, preferred_element_type=jnp.float32)  32.4 us
    ppermute x1, waiting for transfers between devices, shifted(): return lax.ppermute(value, axis, pairs)  26.8 us
  transfers between devices with their start and end apart: 8, of which 7 were waited for; matrix products, arithmetic and copies ran while one was open for 13% of the time, Pallas kernels for 0%

commit v1 on v0

--- a/solution.py
+++ b/solution.py
@@ -71,7 +71,9 @@
     flat_rows = normed.reshape(nchunk * row_count, model_width)
     row_total = nchunk * row_count
     pieces = (
-        lax.all_gather(w_query, "queue", axis=0, tiled=True),
+        jnp.concatenate(
+            lax.all_to_all(jnp.stack([w_query] * lax.axis_size("queue")), "queue", 0, 0), axis=0
+        ),
         lax.all_gather(w_key, "queue", axis=0, tiled=True),
         lax.all_gather(w_value, "queue", axis=0, tiled=True),
     )

time: 835 us -> 773 us (0.926)
  waiting for transfers between devices: 682 us -> 600 us
  starting transfers between devices: 5.76 us -> 16.8 us
    all_gather x1 -> x0, waiting for transfers between devices: 132 us -> none  [shards(): lax.all_gather(w_query, 'queue', axis=0, tiled=True)]
    all_to_all x0 -> x1, waiting for transfers between devices: none -> 79.9 us  [shards(): lax.all_to_all(jnp.stack([w_query] * lax.axis_size('queue')), 'queue', 0, 0)]
    all_gather x1, waiting for transfers between devices: 154 us -> 121 us  [shards(): lax.all_gather(w_key, 'queue', axis=0, tiled=True)]
    all_to_all x0 -> x1, starting transfers between devices: none -> 9.03 us  [shards(): lax.all_to_all(jnp.stack([w_query] * lax.axis_size('queue')), 'queue', 0, 0)]
  transfers between devices with their start and end apart: 8 -> 8, of which waited for: 7 -> 7; matrix products, arithmetic and copies ran while one was open for 13% -> 15% of each run, Pallas kernels for 0% -> 0%
where the time goes in v1:
time: 773 us; the launch traced here: 767 us
  waiting for transfers between devices  600 us (78%)
  matrix products  69.8 us (9%)
  other arithmetic  39.8 us (5%)
  local copies, waits for them, and re-layouts  18.8 us (2%)
  starting transfers between devices  16.8 us (2%)
  between operations  13.6 us (2%)
  blocking collectives  7.96 us (1%)
    all_gather x1, waiting for transfers between devices, shards(): lax.all_gather(w_value, 'queue', axis=0, tiled=True)  162 us
    all_gather x1, waiting for transfers between devices, shards(): lax.all_gather(w_key, 'queue', axis=0, tiled=True)  121 us
    all_gather x1, waiting for transfers between devices, shards(): lax.all_gather(w_out, 'queue', axis=1, tiled=True)  113 us
    reduce_scatter x1, waiting for transfers between devices, shards(): lax.psum_scatter(partial_out.astype(jnp.bfloat16), 'head', scatter_dimens...  83.7 us
    all_to_all x1, waiting for transfers between devices, shards(): lax.all_to_all(jnp.stack([w_query] * lax.axis_size('queue')), 'queue', 0, 0)  79.9 us
    dot_general x3, matrix products, shards(): jnp.dot(flat_rows, piece_rows, preferred_element_type=jnp.float32)  32.4 us
    ppermute x1, waiting for transfers between devices, shifted(): return lax.ppermute(value, axis, pairs)  26.8 us
  transfers between devices with their start and end apart: 8, of which 7 were waited for; matrix products, arithmetic and copies ran while one was open for 15% of the time, Pallas kernels for 0%

profile of v1, /device:TPU:0, one launch (start us, length us, event | category | flops | bytes accessed | tf_op | source)
XLA Modules:
  0.0 766.8 jit_solution(14859837709388380833)
XLA Ops:
  6.5 0.7 all-gather.6.cloned.1.call-update
  7.3 0.7 all-gather.4.cloned.1.call-update
  8.0 4.1 stack.20
  12.1 9.0 %all-to-all-start = ((bf16[32,160,640]{2,1,0:T(8,128)(2,1)}), bf16[32,160,640]{2,1,0:T(8,128)(2,1)}, u32[]{:S(2)}, u32[]{:S(2)}) async-start(bf16[32,160,640]{2,1,0:T(8,128)(2,1)} %stack.20), calls=%async_computation | async-start | bytes 13107200 | tf_op jit(solution)/shard_map/all_to_all | solution.py:75
  21.2 0.7 all-gather.8.cloned.1.call-update
  21.9 0.1 pad.8.clone
  22.0 0.1 compare_and_fusion.1
  22.1 0.1 add_add_fusion
  22.2 13.6 %convert_add_fusion = (f32[2,384,5120]{2,1,0:T(8,128)}, f32[2,384]{1,0:T(2,128)S(1)}) fusion(bf16[2,384,5120]{2,1,0:T(8,128)(2,1)} %param.12, bf16[2,384,5120]{2,1,0:T(8,128)(2,1)} %param.11), kind=kLoop, calls=%fused_computation.6 | loop fusion | flops 15727872 | bytes 31460352 | tf_op jit(solution)/shard_map/add | solution.py:61
  35.8 6.4 multiply_reduce_fusion
  42.2 3.5 fusion.6
  45.7 9.6 %add_convert_fusion = bf16[2,384,5120]{2,1,0:T(8,128)(2,1)} fusion(f32[2,5120]{1,0:T(2,128)S(1)} %get-tuple-element.14, f32[2,5120]{1,0:T(2,128)S(1)} %get-tuple-element.15, f32[2,384]{1,0:T(2,128)S(1)} %add_rsqrt_fusion.2, f32[2,384]{1,0:T(2,128)S(1)} %broadcast_multiply_fusion, bf16[2,384,5120]{2,1,0:T(8,128)(2,1)S(1)} %bitcast.59, ...), kind=kLoop, calls=%fused_computation.4 | loop fusion | flops 31457280 | bytes 23681024 | tf_op jit(solution)/shard_map/convert_element_type | solution.py:70
  55.3 79.9 %all-to-all-done = bf16[32,160,640]{2,1,0:T(8,128)(2,1)} async-done(((bf16[32,160,640]{2,1,0:T(8,128)(2,1)}), bf16[32,160,640]{2,1,0:T(8,128)(2,1)}, u32[]{:S(2)}, u32[]{:S(2)}) %all-to-all-start) | async-done | bytes 6553632 | tf_op jit(solution)/shard_map/all_to_all | solution.py:75
  135.2 10.5 %fusion.17 = (f32[768]{0:T(1024)S(1)}, bf16[768,640]{0,1:T(8,128)(2,1)S(1)}) fusion(bf16[768,5120]{1,0:T(8,128)(2,1)} %bitcast.60, bf16[5120,640]{1,0:T(8,128)(2,1)} %bitcast.8), kind=kOutput, calls=%fused_computation.30 | convolution fusion | flops 5035129856 | bytes 15404032 | tf_op jit(solution)/shard_map/dot_general | solution.py:82
  145.7 120.5 %all-gather.6.cloned.1.call-done = bf16[5120,640]{1,0:T(8,128)(2,1)} async-done(((bf16[160,640]{1,0:T(8,128)(2,1)}), bf16[5120,640]{1,0:T(8,128)(2,1)}) %all-gather.6.cloned.1.call-update) | async-done | bytes 6553616 | tf_op jit(solution)/shard_map/all_gather | solution.py:77
  266.3 10.6 %fusion.20 = (f32[768]{0:T(1024)S(1)}, bf16[768,640]{1,0:T(8,128)(2,1)S(1)}) fusion(bf16[768,5120]{1,0:T(8,128)(2,1)} %bitcast.61, bf16[5120,640]{1,0:T(8,128)(2,1)} %all-gather.6.cloned.1.call-done), kind=kOutput, calls=%fused_computation.33 | convolution fusion | flops 5035129856 | bytes 15404032 | tf_op jit(solution)/shard_map/dot_general | solution.py:82
  276.9 8.0 %all-reduce = (f32[768]{0:T(1024)S(1)}, f32[768]{0:T(1024)S(1)}) all-reduce(f32[768]{0:T(1024)S(1)} %get-tuple-element.18, f32[768]{0:T(1024)S(1)} %get-tuple-element.20), channel_id=1, replica_groups=mesh['queue'=32,'head'=4] {'head'}, use_global_device_ids=true, to_apply=%region_5.0 | all-reduce | flops 1536 | bytes 12288 | tf_op jit(solution)/shard_map/psum | solution.py:89
  284.9 0.3 fusion.22
  285.3 3.1 collective-permute-start.1
  288.4 162.1 %all-gather.4.cloned.1.call-done = bf16[5120,640]{1,0:T(8,128)(2,1)} async-done(((bf16[160,640]{1,0:T(8,128)(2,1)}), bf16[5120,640]{1,0:T(8,128)(2,1)}) %all-gather.4.cloned.1.call-update) | async-done | bytes 6553616 | tf_op jit(solution)/shard_map/all_gather | solution.py:78
  450.5 11.3 %convolution_convert_fusion.3 = bf16[768,640]{1,0:T(8,128)(2,1)} fusion(bf16[768,5120]{1,0:T(8,128)(2,1)} %bitcast.62, bf16[5120,640]{1,0:T(8,128)(2,1)} %all-gather.4.cloned.1.call-done), kind=kOutput, calls=%fused_computation.48 | convolution fusion | flops 5033656320 | bytes 15400960 | tf_op jit(solution)/shard_map/dot_general | solution.py:82
  461.7 3.7 collective-permute-start
  465.5 0.1 broadcast_bitcast_fusion
  465.6 0.3 fusion.19
  465.9 1.2 reshape.91
  467.1 2.0 fusion.27
  469.1 2.1 copy.21
  471.2 3.6 copy.23
  474.8 0.9 copy.22
  475.8 2.1 copy.24
  477.9 12.4 %collective-permute-done = bf16[768,640]{1,0:T(8,128)(2,1)} collective-permute-done((bf16[768,640]{1,0:T(8,128)(2,1)}, bf16[768,640]{1,0:T(8,128)(2,1)}, u32[]{:S(2)}, u32[]{:S(2)}) %collective-permute-start) | collective-permute-done | bytes 983072 | tf_op jit(solution)/shard_map/ppermute | solution.py:12
  490.3 2.0 fusion.28
  492.3 2.2 copy.19
  494.5 0.9 copy.20
  495.5 14.5 %fusion.56 = (f32[2,5,384]{2,1,0:T(8,128)S(1)}, f32[2,5,384,1152]{3,2,1,0:T(8,128)}) fusion(pred[2,1152]{1,0:T(4,128)(4,1)S(1)} %bitcast.70, bf16[1,1152,5,128]{3,1,2,0:T(8,128)(2,1)} %copy.24, bf16[1,1152,5,128]{3,1,2,0:T(8,128)(2,1)} %copy.23, bf16[2,384,5,128]{1,0,3,2:T(2,128)(2,1)} %reshape.91), kind=kOutput, calls=%fused_computation.78 | convolution fusion | flops 1151632512 | bytes 21644544 | tf_op jit(solution)/shard_map/sub | solution.py:122
  510.0 7.8 %fusion.32 = bf16[2,384,5,128]{1,3,2,0:T(8,128)(2,1)S(1)} fusion(f32[2,5,384,1152]{3,2,1,0:T(8,128)} %get-tuple-element.23, f32[2,5,384]{2,1,0:T(8,128)S(1)} %get-tuple-element.22, bf16[1,1152,5,128]{1,3,2,0:T(8,128)(2,1)S(1)} %bitcast.68, bf16[1,1152,5,128]{1,3,2,0:T(8,128)(2,1)S(1)} %bitcast.67), kind=kOutput, calls=%fused_computation.49 | convolution fusion | flops 1143275520 | bytes 21642240 | tf_op jit(solution)/shard_map/chqk,ckhd->cqhd/dot_general | solution.py:124
  517.8 1.0 copy.26
  518.8 0.2 copy.30
  519.0 112.6 %all-gather.8.cloned.1.call-done = bf16[640,5120]{0,1:T(8,128)(2,1)} async-done(((bf16[640,160]{0,1:T(8,128)(2,1)}), bf16[640,5120]{0,1:T(8,128)(2,1)}) %all-gather.8.cloned.1.call-update) | async-done | bytes 6553616 | tf_op jit(solution)/shard_map/all_gather | solution.py:130
  631.5 11.6 %convolution_convert_fusion = bf16[768,5120]{1,0:T(8,128)(2,1)} fusion(bf16[768,640]{0,1:T(8,128)(2,1)S(1)} %bitcast.69, bf16[640,5120]{0,1:T(8,128)(2,1)} %all-gather.8.cloned.1.call-done), kind=kOutput, calls=%fused_computation.12 | convolution fusion | flops 5037096960 | bytes 15400960 | tf_op jit(solution)/shard_map/dot_general | solution.py:128
  643.2 83.7 %reduce-scatter.2.cloned.1.call-done = bf16[768,1280]{1,0:T(8,128)(2,1)} async-done(((bf16[768,5120]{1,0:T(8,128)(2,1)}), bf16[768,1280]{1,0:T(8,128)(2,1)}) %reduce-scatter.2.cloned.1.call-update) | async-done | bytes 1966096 | tf_op jit(solution)/shard_map/reduce_scatter | solution.py:137
  726.9 3.1 fusion.9
  730.0 0.1 fusion.35
  730.1 0.7 collective-permute-start.2
  730.8 0.1 slice.57
  730.9 26.8 %collective-permute-done.2 = bf16[384,1280]{1,0:T(8,128)(2,1)S(1)} collective-permute-done((bf16[384,1280]{1,0:T(8,128)(2,1)S(1)}, bf16[384,1280]{1,0:T(8,128)(2,1)S(1)}, u32[]{:S(2)}, u32[]{:S(2)}) %collective-permute-start.2) | collective-permute-done | bytes 983072 | tf_op jit(solution)/shard_map/ppermute | solution.py:18
  757.7 0.1 bitcast_convert_fusion
  757.8 2.2 pad_maximum_fusion
  (30 shorter events, 0.3 us)
Async XLA Ops:
  6.5 259.8 %all-gather.6.cloned.1.call-start = ((), (), s32[]{:S(2)}) async-start(), calls=%async_computation.3 | async-start | bytes 6758400 | tf_op jit(solution)/shard_map/all_gather | solution.py:77
  7.3 443.2 %all-gather.4.cloned.1.call-start = ((), (), s32[]{:S(2)}) async-start(), calls=%async_computation.2 | async-start | bytes 6758400 | tf_op jit(solution)/shard_map/all_gather | solution.py:78
  12.1 9.9 %copy-start.4 = (s32[2,2]{1,0:T(2,128)S(1)}, s32[2,2]{1,0:T(2,128)}, u32[]{:S(2)}) copy-start(s32[2,2]{1,0:T(2,128)} %param.14) | copy-start | bytes 52
  12.1 123.1 %all-to-all-start = ((bf16[32,160,640]{2,1,0:T(8,128)(2,1)}), bf16[32,160,640]{2,1,0:T(8,128)(2,1)}, u32[]{:S(2)}, u32[]{:S(2)}) async-start(bf16[32,160,640]{2,1,0:T(8,128)(2,1)} %stack.20), calls=%async_computation | async-start | bytes 13107200 | tf_op jit(solution)/shard_map/all_to_all | solution.py:75
  21.2 610.4 %all-gather.8.cloned.1.call-start = ((), (), s32[]{:S(2)}) async-start(), calls=%async_computation.4 | async-start | bytes 6758400 | tf_op jit(solution)/shard_map/all_gather | solution.py:130
  21.9 705.0 %reduce-scatter.2.cloned.1.call-start = ((), (), s32[]{:S(2)}) async-start(), calls=%async_computation.5 | async-start | bytes 9830400 | tf_op jit(solution)/shard_map/reduce_scatter | solution.py:137
  22.1 13.7 %slice-start = ((s8[7864320]{0:T(1024)(128)(4,1)}), s8[4194304]{0:T(1024)(128)(4,1)S(1)}, s32[]{:S(2)}) async-start(s8[7864320]{0:T(1024)(128)(4,1)} %bitcast.58), calls=%async_computation.6 | async-start | bytes 8388608
  22.2 13.6 %slice-start.1 = ((s8[7864320]{0:T(1024)(128)(4,1)}), s8[3670016]{0:T(1024)(128)(4,1)S(1)}, s32[]{:S(2)}) async-start(s8[7864320]{0:T(1024)(128)(4,1)} %bitcast.58), calls=%async_computation.7 | async-start | bytes 7340032
  35.8 6.4 copy-start.5
  145.7 139.2 %copy-start.2 = (f32[640]{0:T(1024)S(1)}, f32[640]{0:T(1024)}, u32[]{:S(2)}) copy-start(f32[640]{0:T(1024)} %param.21) | copy-start | bytes 7684
  285.2 176.5 %copy-start = (bf16[768,640]{1,0:T(8,128)(2,1)}, bf16[768,640]{1,0:T(8,128)(2,1)S(1)}, u32[]{:S(2)}) copy-start(bf16[768,640]{1,0:T(8,128)(2,1)S(1)} %fusion.22) | copy-start | bytes 2949124
  285.2 180.3 %copy-start.3 = (f32[640]{0:T(1024)S(1)}, f32[640]{0:T(1024)}, u32[]{:S(2)}) copy-start(f32[640]{0:T(1024)} %param.20) | copy-start | bytes 7684
  285.3 181.8 %collective-permute-start.1 = (bf16[768,640]{1,0:T(8,128)(2,1)S(1)}, bf16[768,640]{1,0:T(8,128)(2,1)}, u32[]{:S(2)}, u32[]{:S(2)}) collective-permute-start(bf16[768,640]{1,0:T(8,128)(2,1)S(1)} %fusion.22), channel_id=1, source_target_pairs={{0,4},{4,8},{8,12},{12,16},{16,20},{20,24},{24,28},{28,32},{32,36}... | collective-permute-start | bytes 2949128 | tf_op jit(solution)/shard_map/ppermute | solution.py:12
  461.7 28.6 %collective-permute-start = (bf16[768,640]{1,0:T(8,128)(2,1)}, bf16[768,640]{1,0:T(8,128)(2,1)}, u32[]{:S(2)}, u32[]{:S(2)}) collective-permute-start(bf16[768,640]{1,0:T(8,128)(2,1)} %convolution_convert_fusion.3), channel_id=1, source_target_pairs={{0,4},{4,8},{8,12},{12,16},{16,20},{20,24},{24,28},{28,32},{32,36}... | collective-permute-start | bytes 2949128 | tf_op jit(solution)/shard_map/ppermute | solution.py:12
  495.5 14.6 %copy-start.1 = (bf16[1152,640]{0,1:T(8,128)(2,1)S(1)}, bf16[1152,640]{0,1:T(8,128)(2,1)}, u32[]{:S(2)}) copy-start(bf16[1152,640]{0,1:T(8,128)(2,1)} %copy.19) | copy-start | bytes 4423684
  730.1 27.6 %collective-permute-start.2 = (bf16[384,1280]{1,0:T(8,128)(2,1)S(1)}, bf16[384,1280]{1,0:T(8,128)(2,1)S(1)}, u32[]{:S(2)}, u32[]{:S(2)}) collective-permute-start(bf16[384,1280]{1,0:T(8,128)(2,1)S(1)} %fusion.35), channel_id=1, source_target_pairs={{0,4},{4,8},{8,12},{12,16},{16,20},{20,24},{24,28},{28,32},{32,36}... | collective-permute-start | bytes 2949128 | tf_op jit(solution)/shard_map/ppermute | solution.py:18
Sparse Core Ops, SparseCore 0:
  9.0 257.2 all-gather.5
  267.9 182.4 all-gather.3
  452.1 179.3 all-gather.7
  643.3 83.5 reduce-scatter.1
